TPU v7x, 512 devices: a whole 4x8x8 slice. The times are simulated.
512 devices in a mesh: dp: 8 (over x, y_hi), seq: 64 (over z, y_lo, core).
Axes of the slice: x: 4, y: 8 (y_hi: 2, y_lo: 4; y = y_hi * 4 + y_lo), z: 8, core: 2. Of those that a mesh axis runs over, the one named last changes fastest.
Arguments:
- points: bfloat16 [8, 16384, 384], P('dp', 'seq'), may hold values from -6 to 6
- cotangent: bfloat16 [8, 16384, 384], P('dp', 'seq'), may hold values from -6 to 6
- in_gain: float32 [384], replicated, may hold values from 0.5 to 2
- out_gain: float32 [384], replicated, may hold values from 0.5 to 2
- left_factor: bfloat16 [256, 256], replicated, may hold values from -0.375 to 0.375
- right_factor: bfloat16 [64, 64], replicated, may hold values from -0.75 to 0.75
- norm_gain: float32 [384], replicated, may hold values from 0.5 to 2
- gate_weight: bfloat16 [4, 96, 384], P(None, None, 'dp'), may hold values from -0.625 to 0.625
- up_weight: bfloat16 [4, 96, 384], P(None, None, 'dp'), may hold values from -0.625 to 0.625
- down_weight: bfloat16 [4, 96, 384], P(None, None, 'dp'), may hold values from -0.3125 to 0.3125
Outputs:
- layer_out: bfloat16 [8, 16384, 384], P('dp', 'seq')
- grad_points: bfloat16 [8, 16384, 384], P('dp', 'seq')
- grad_left: float32 [256, 256], replicated
- grad_right: float32 [64, 64], replicated
- grad_in_gain: float32 [384], replicated
- grad_out_gain: float32 [384], replicated
- grad_norm_gain: float32 [384], replicated
- grad_gate: float32 [4, 96, 384], P(None, None, 'dp')
- grad_up: float32 [4, 96, 384], P(None, None, 'dp')
- grad_down: float32 [4, 96, 384], P(None, None, 'dp')
All inputs are finite; a program needn't handle non-finite values.
Results may differ from a plain program's by a relative error of at most 0.0091.
Values may be sent and summed in bfloat16 or wider, within the bound.
A program may use at most 64 MiB of HBM per device.

v0:
```python
import jax
import jax.numpy as jnp
from jax import lax
from jax.sharding import PartitionSpec as P


def shards(
    points,
    cotangent,
    in_gain,
    out_gain,
    left_factor,
    right_factor,
    norm_gain,
    gate_weight,
    up_weight,
    down_weight,
):
    seq_count = lax.axis_size("seq")
    data_count = lax.axis_size("dp")
    row_count = points.shape[1]
    channels = points.shape[2]
    block_size = left_factor.shape[0]
    block_total = right_factor.shape[0]
    blocks = row_count // block_size
    shard_width = gate_weight.shape[2]
    gate_full, up_full, down_full = (
        lax.all_gather(gate_weight, "dp", axis=2, tiled=True),
        lax.all_gather(up_weight, "dp", axis=2, tiled=True),
        lax.all_gather(down_weight, "dp", axis=2, tiled=True),
    )
    nblocks = gate_full.shape[0]
    block_in = gate_full.shape[1]
    block_hidden = gate_full.shape[2]
    quarter = block_hidden // nblocks
    inputs = points[0].astype(jnp.float32)
    scaled = (inputs * in_gain).astype(jnp.bfloat16).reshape(blocks, block_size, channels)
    first_mix = jnp.einsum(
        "pb,abc->apc", left_factor, scaled, preferred_element_type=jnp.float32
    ).astype(jnp.bfloat16)
    received = lax.all_to_all(first_mix, "seq", split_axis=1, concat_axis=0, tiled=True)
    mixed = jnp.einsum("qa,apc->pqc", right_factor, received, preferred_element_type=jnp.float32)
    first_moved = received
    mixed = mixed.reshape(row_count, channels)
    residual = inputs + out_gain * mixed
    inv_rms = lax.rsqrt(jnp.mean(residual * residual, axis=-1, keepdims=True) + 1e-05)
    normed = residual * inv_rms
    hidden_in = (normed * norm_gain).astype(jnp.bfloat16).reshape(row_count, nblocks, block_in)
    gate_pre = jnp.einsum("rkd,kdf->rkf", hidden_in, gate_full, preferred_element_type=jnp.float32)
    up_pre = jnp.einsum("rkd,kdf->rkf", hidden_in, up_full, preferred_element_type=jnp.float32)
    sig_gate = jax.nn.sigmoid(gate_pre)
    act_gate = gate_pre * sig_gate
    hidden = (act_gate * up_pre).astype(jnp.bfloat16)
    hidden_grid = hidden.reshape(row_count, nblocks, nblocks, quarter)
    down_grid = down_full.reshape(nblocks, block_in, nblocks, quarter)
    branch = jnp.einsum(
        "rkjf,jokf->rjo", hidden_grid, down_grid, preferred_element_type=jnp.float32
    ).reshape(row_count, channels)
    layer_out = (residual + branch).astype(jnp.bfloat16)
    grad_grid = cotangent[0].reshape(row_count, nblocks, block_in)
    dhidden = jnp.einsum(
        "rjo,jokf->rkjf", grad_grid, down_grid, preferred_element_type=jnp.float32
    ).reshape(row_count, nblocks, block_hidden)
    grad_down = jnp.einsum(
        "rjo,rkjf->jokf", grad_grid, hidden_grid, preferred_element_type=jnp.float32
    ).reshape(nblocks, block_in, block_hidden)
    dgate = (dhidden * up_pre * sig_gate * (1.0 + gate_pre * (1.0 - sig_gate))).astype(jnp.bfloat16)
    dupper = (dhidden * act_gate).astype(jnp.bfloat16)
    dhid_in = jnp.einsum("rkf,kdf->rkd", dgate, gate_full, preferred_element_type=jnp.float32)
    dhid_in = (
        dhid_in + jnp.einsum("rkf,kdf->rkd", dupper, up_full, preferred_element_type=jnp.float32)
    ).reshape(row_count, channels)
    grad_gate = jnp.einsum("rkd,rkf->kdf", hidden_in, dgate, preferred_element_type=jnp.float32)
    grad_up = jnp.einsum("rkd,rkf->kdf", hidden_in, dupper, preferred_element_type=jnp.float32)
    grad_norm = jnp.sum(dhid_in * normed, axis=0)
    scaled_grad = dhid_in * norm_gain
    dresid = cotangent[0].astype(jnp.float32) + inv_rms * (
        scaled_grad - normed * jnp.mean(scaled_grad * normed, axis=-1, keepdims=True)
    )
    grad_out = jnp.sum(dresid * mixed, axis=0)
    dmixed = (
        (dresid * out_gain)
        .astype(jnp.bfloat16)
        .reshape(block_size // seq_count, block_total, channels)
    )
    dfirst = jnp.einsum(
        "qa,pqc->apc", right_factor, dmixed, preferred_element_type=jnp.float32
    ).astype(jnp.bfloat16)
    grad_right = jnp.einsum("pqc,apc->qa", dmixed, first_moved, preferred_element_type=jnp.float32)
    received = lax.all_to_all(dfirst, "seq", split_axis=0, concat_axis=1, tiled=True)
    dscaled = jnp.einsum("pb,apc->abc", left_factor, received, preferred_element_type=jnp.float32)
    grad_left = jnp.einsum("apc,abc->pb", received, scaled, preferred_element_type=jnp.float32)
    dscaled = dscaled.reshape(row_count, channels)
    grad_in = jnp.sum(dscaled * inputs, axis=0)
    grad_points = (dresid + dscaled * in_gain).astype(jnp.bfloat16)
    factor = float(data_count * row_count * seq_count) ** (-0.5)
    totals = lax.psum(
        (grad_gate, grad_up, grad_down, grad_left, grad_right, grad_in, grad_out, grad_norm),
        ("dp", "seq"),
    )
    start = lax.axis_index("dp") * shard_width
    gate_sum = lax.dynamic_slice_in_dim(totals[0], start, shard_width, 2)
    up_sum = lax.dynamic_slice_in_dim(totals[1], start, shard_width, 2)
    down_sum = lax.dynamic_slice_in_dim(totals[2], start, shard_width, 2)
    left_sum, right_sum, in_sum, out_sum, norm_sum = (
        totals[3],
        totals[4],
        totals[5],
        totals[6],
        totals[7],
    )
    return (
        layer_out[None],
        grad_points[None],
        left_sum * factor,
        right_sum * factor,
        in_sum * factor,
        out_sum * factor,
        norm_sum * factor,
        gate_sum * factor,
        up_sum * factor,
        down_sum * factor,
    )


def solution(mesh):
    in_specs = (
        P("dp", "seq", None),
        P("dp", "seq", None),
        P(),
        P(),
        P(),
        P(),
        P(),
        P(None, None, "dp"),
        P(None, None, "dp"),
        P(None, None, "dp"),
    )
    out_specs = (
        P("dp", "seq", None),
        P("dp", "seq", None),
        P(),
        P(),
        P(),
        P(),
        P(),
        P(None, None, "dp"),
        P(None, None, "dp"),
        P(None, None, "dp"),
    )
    return jax.shard_map(shards, mesh=mesh, in_specs=in_specs, out_specs=out_specs, check_vma=False)
```

profile of v0, /device:TPU:17, one launch (start us, length us, event | category | flops | bytes accessed | tf_op | source)
XLA Modules:
  0.0 500.2 jit_solution(1939229281374899762)
XLA Ops:
  7.2 0.9 copy-done
  8.1 1.2 fusion.8
  9.3 0.5 copy.58
  9.7 0.5 broadcast.185
  10.3 1.8 reduce.5
  12.1 0.8 reshape.326
  12.9 14.7 %all-to-all-start = ((bf16[64,2,768]{2,1,0:T(2,128)(2,1)}), bf16[64,2,768]{2,1,0:T(2,128)(2,1)}, u32[]{:S(2)}, u32[]{:S(2)}) async-start(bf16[64,2,768]{2,1,0:T(2,128)(2,1)} %reshape.326), calls=%async_computation | async-start | bytes 393216 | tf_op jit(solution)/shard_map/all_to_all | solution.py:41
  27.6 42.0 %all_gather.11 = bf16[4,96,384]{1,2,0:T(8,128)(2,1)S(1)} all-gather(bf16[4,96,48]{1,2,0:T(8,128)(2,1)S(1)} %copy-done.15), channel_id=1, replica_groups=mesh['dp'=8,'seq'=64] {'dp'}, dimensions={2}, use_global_device_ids=true | all-gather | bytes 331776 | tf_op jit(solution)/shard_map/all_gather | solution.py:30
  69.8 0.3 convolution_bitcast_fusion
  70.2 0.9 copy.60
  71.1 0.8 convert_element_type.81
  72.2 1.6 copy.69
  73.8 38.9 %all_gather.10 = bf16[4,96,384]{1,2,0:T(8,128)(2,1)S(1)} all-gather(bf16[4,96,48]{1,2,0:T(8,128)(2,1)S(1)} %copy-done.16), channel_id=1, replica_groups=mesh['dp'=8,'seq'=64] {'dp'}, dimensions={2}, use_global_device_ids=true | all-gather | bytes 331776 | tf_op jit(solution)/shard_map/all_gather | solution.py:29
  112.7 40.8 %all_gather.9 = bf16[4,96,384]{1,2,0:T(8,128)(2,1)S(1)} all-gather(bf16[4,96,48]{1,2,0:T(8,128)(2,1)S(1)} %copy-done.17), channel_id=1, replica_groups=mesh['dp'=8,'seq'=64] {'dp'}, dimensions={2}, use_global_device_ids=true | all-gather | bytes 331776 | tf_op jit(solution)/shard_map/all_gather | solution.py:28
  153.6 1.5 reshape.327
  155.1 1.1 bitcast_reduce_fusion
  156.7 0.3 reshape.305
  157.0 0.2 copy.61
  157.5 0.4 fusion.30
  157.9 0.8 copy-done.8
  158.7 2.0 multiply_convert_fusion
  160.7 0.4 fusion.31
  161.1 1.3 fusion.32
  162.4 1.3 fusion.33
  163.7 0.5 multiply_reduce_fusion
  164.2 0.9 copy.71
  165.2 0.3 copy.62
  165.5 0.3 fusion.19
  165.8 0.9 copy.65
  166.8 0.2 copy.72
  167.1 0.3 reshape.312
  167.4 1.2 multiply_reduce_fusion.1
  168.6 0.2 fusion.9
  168.9 0.8 copy.74
  169.7 25.1 %all-to-all-start.1 = ((bf16[64,4,384]{2,1,0:T(4,128)(2,1)}), bf16[64,4,384]{2,1,0:T(4,128)(2,1)S(1)}, u32[]{:S(2)}, u32[]{:S(2)}) async-start(bf16[64,4,384]{2,1,0:T(4,128)(2,1)} %copy.74), calls=%async_computation.1 | async-start | bytes 393216 | tf_op jit(solution)/shard_map/all_to_all | solution.py:90
  195.0 0.2 convolution_bitcast_fusion.1
  195.2 1.2 fusion.10
  196.4 8.6 %all-to-all-done.1 = bf16[64,4,384]{2,1,0:T(4,128)(2,1)S(1)} async-done(((bf16[64,4,384]{2,1,0:T(4,128)(2,1)}), bf16[64,4,384]{2,1,0:T(4,128)(2,1)S(1)}, u32[]{:S(2)}, u32[]{:S(2)}) %all-to-all-start.1) | async-done | bytes 196640 | tf_op jit(solution)/shard_map/all_to_all | solution.py:90
  205.1 1.0 fusion.25
  206.2 1.0 fusion.18
  207.3 98.6 %all-reduce = (f32[64,64]{1,0:T(8,128)S(1)}, f32[384]{0:T(512)S(1)}, f32[384]{0:T(512)S(1)}, f32[384]{0:T(512)S(1)}) all-reduce(f32[64,64]{1,0:T(8,128)S(1)} %convolution_bitcast_fusion.1, f32[384]{0:T(512)S(1)} %fusion.12, f32[384]{0:T(512)S(1)} %get-tuple-element.20, ...), channel_id=1, replica_groups=mesh['dp'=8,'seq'=64] {'dp','seq'}, use_global_device_ids=true, to_apply=%region_3.0 | all-reduce | flops 5248 | bytes 41984 | tf_op jit(solution)/shard_map/psum | solution.py:97
  305.9 0.6 broadcast_multiply_fusion.4
  306.5 0.6 broadcast_multiply_fusion.2
  307.0 0.6 broadcast_multiply_fusion.1
  307.7 180.8 %all-reduce.4.cloned.1.call-done = (f32[256,256]{1,0:T(8,128)}, f32[4,96,384]{1,2,0:T(8,128)}, f32[4,96,384]{1,2,0:T(8,128)}, f32[4,96,384]{1,2,0:T(8,128)}) async-done(((f32[256,256]{1,0:T(8,128)}, f32[4,96,384]{1,2,0:T(8,128)}, f32[4,96,384]{1,2,0:T(8,128)}, f32[4,96,384]{1,2,0:T(8,128)}), (f32[256,256]{1,0:T(8,128)}, f32[4,96,384]{1,2,0:T(8,128)}, f32[4,96,384]{1,2,0:T(8,128)}, ...) | async-done | bytes 2031632 | tf_op jit(solution)/shard_map/psum | solution.py:97
  488.5 1.7 broadcast_multiply_fusion
  490.2 1.5 dynamic-slice_multiply_fusion.2
  491.7 1.6 dynamic-slice_multiply_fusion
  (56 shorter events, 1.6 us)
Async XLA Ops:
  7.2 0.9 copy-start
  7.2 20.4 %copy-start.15 = (bf16[4,96,48]{1,2,0:T(8,128)(2,1)S(1)}, bf16[4,96,48]{1,2,0:T(8,128)(2,1)}, u32[]{:S(2)}) copy-start(bf16[4,96,48]{1,2,0:T(8,128)(2,1)} %param.19) | copy-start | bytes 110596
  7.2 62.4 %copy-start.6 = (bf16[1,256,384]{2,1,0:T(8,128)(2,1)S(1)}, bf16[1,256,384]{2,1,0:T(8,128)(2,1)}, u32[]{:S(2)}) copy-start(bf16[1,256,384]{2,1,0:T(8,128)(2,1)} %param.11) | copy-start | bytes 589828
  12.9 140.7 %all-to-all-start = ((bf16[64,2,768]{2,1,0:T(2,128)(2,1)}), bf16[64,2,768]{2,1,0:T(2,128)(2,1)}, u32[]{:S(2)}, u32[]{:S(2)}) async-start(bf16[64,2,768]{2,1,0:T(2,128)(2,1)} %reshape.326), calls=%async_computation | async-start | bytes 393216 | tf_op jit(solution)/shard_map/all_to_all | solution.py:41
  27.6 42.6 %copy-start.1 = (bf16[1,256,384]{2,1,0:T(8,128)(2,1)S(1)}, bf16[1,256,384]{2,1,0:T(8,128)(2,1)}, u32[]{:S(2)}) copy-start(bf16[1,256,384]{2,1,0:T(8,128)(2,1)} %param.10) | copy-start | bytes 589828
  69.6 1.4 copy-start.2
  69.8 2.1 copy-start.4
  69.8 2.1 copy-start.19
  69.8 2.1 copy-start.13
  72.2 1.7 copy-start.16
  72.2 40.5 %copy-start.17 = (bf16[4,96,48]{1,2,0:T(8,128)(2,1)S(1)}, bf16[4,96,48]{1,2,0:T(8,128)(2,1)}, u32[]{:S(2)}) copy-start(bf16[4,96,48]{1,2,0:T(8,128)(2,1)} %param.17) | copy-start | bytes 110596
  73.8 82.5 %copy-start.14 = (bf16[64,64]{1,0:T(8,128)(2,1)S(1)}, bf16[64,64]{1,0:T(8,128)(2,1)}, u32[]{:S(2)}) copy-start(bf16[64,64]{1,0:T(8,128)(2,1)} %param.15) | copy-start | bytes 24580
  156.3 1.0 copy-start.9
  157.3 1.4 copy-start.8
  163.7 1.5 copy-start.12
  164.2 1.2 copy-start.3
  165.8 1.5 copy-start.7
  167.3 27.8 %copy-start.5 = (bf16[1,256,384]{1,2,0:T(8,128)(2,1)S(1)}, bf16[1,256,384]{1,2,0:T(8,128)(2,1)}, u32[]{:S(2)}) copy-start(bf16[1,256,384]{1,2,0:T(8,128)(2,1)} %copy-done.4) | copy-start | bytes 589828
  169.7 35.3 %copy-start.18 = (f32[384]{0:T(512)S(1)}, f32[384]{0:T(512)}, u32[]{:S(2)}) copy-start(f32[384]{0:T(512)} %param.12) | copy-start | bytes 4612
  169.7 35.3 %all-to-all-start.1 = ((bf16[64,4,384]{2,1,0:T(4,128)(2,1)}), bf16[64,4,384]{2,1,0:T(4,128)(2,1)S(1)}, u32[]{:S(2)}, u32[]{:S(2)}) async-start(bf16[64,4,384]{2,1,0:T(4,128)(2,1)} %copy.74), calls=%async_computation.1 | async-start | bytes 393216 | tf_op jit(solution)/shard_map/all_to_all | solution.py:90
  194.8 293.7 %all-reduce.4.cloned.1.call-start = ((), (), s32[]{:S(2)}) async-start(), calls=%async_computation.2 | async-start | bytes 5242880 | tf_op jit(solution)/shard_map/psum | solution.py:97
  205.0 1.0 copy-start.10
  205.1 1.1 copy-start.11
Sparse Core Ops, SparseCore 0:
  206.2 282.2 all-reduce.3
where the time goes:
time: 501 us; the launch traced here: 500 us
  blocking collectives  220 us (44%)
  waiting for transfers between devices  189 us (38%)
  starting transfers between devices  39.9 us (8%)
  between operations  14.4 us (3%)
  local copies, waits for them, and re-layouts  13.6 us (3%)
  matrix products  11.6 us (2%)
  other arithmetic  10.9 us (2%)
    psum x1, waiting for transfers between devices, shards(): lax.psum((grad_gate, grad_up, grad_down, grad_left, grad_right, grad_in,...  181 us
    psum x1, blocking collectives, shards(): lax.psum((grad_gate, grad_up, grad_down, grad_left, grad_right, grad_in,...  98.6 us
    all_gather x1, blocking collectives, shards(): lax.all_gather(down_weight, 'dp', axis=2, tiled=True)  42 us
    all_gather x1, blocking collectives, shards(): lax.all_gather(gate_weight, 'dp', axis=2, tiled=True)  40.8 us
    all_gather x1, blocking collectives, shards(): lax.all_gather(up_weight, 'dp', axis=2, tiled=True)  38.9 us
    all_to_all x1, starting transfers between devices, shards(): lax.all_to_all(dfirst, 'seq', split_axis=0, concat_axis=1, tiled=True)  25.1 us
    all_to_all x1, starting transfers between devices, shards(): lax.all_to_all(first_mix, 'seq', split_axis=1, concat_axis=0, tiled=True)  14.7 us
  transfers between devices with their start and end apart: 3, of which 2 were waited for; matrix products, arithmetic and copies ran while one was open for 2% of the time, Pallas kernels for 0%

commit v1 on v0

--- a/solution.py
+++ b/solution.py
@@ -2,6 +2,13 @@
 import jax.numpy as jnp
 from jax import lax
 from jax.sharding import PartitionSpec as P
+from jax.lax import all_to_all, axis_size
+
+
+def track_the_spans(buf, mesh_dim):
+    formed = jnp.stack([buf for _ in range(axis_size(mesh_dim))])
+    reached = all_to_all(formed, axis_name=mesh_dim, split_axis=0, concat_axis=0)
+    return jnp.concatenate(reached, axis=2)
 
 
 def shards(
@@ -25,7 +32,7 @@
     blocks = row_count // block_size
     shard_width = gate_weight.shape[2]
     gate_full, up_full, down_full = (
-        lax.all_gather(gate_weight, "dp", axis=2, tiled=True),
+        track_the_spans(gate_weight, "dp"),
         lax.all_gather(up_weight, "dp", axis=2, tiled=True),
         lax.all_gather(down_weight, "dp", axis=2, tiled=True),
     )

time: 501 us -> 471 us (0.940)
  blocking collectives: 220 us -> 176 us
  starting transfers between devices: 39.9 us -> 46.2 us
    all_gather x1 -> x0, blocking collectives: 40.8 us -> none  [shards(): lax.all_gather(gate_weight, 'dp', axis=2, tiled=True)]
    all_to_all x0 -> x1, starting transfers between devices: none -> 6.61 us  [track_the_spans(): all_to_all(formed, axis_name=mesh_dim, split_axis=0, concat_axis=0)]
    all_to_all x0 -> x1, waiting for transfers between devices: none -> 5.88 us  [track_the_spans(): all_to_all(formed, axis_name=mesh_dim, split_axis=0, concat_axis=0)]
  transfers between devices with their start and end apart: 3 -> 4, of which waited for: 2 -> 3; matrix products, arithmetic and copies ran while one was open for 2% -> 3% of each run, Pallas kernels for 0% -> 0%
where the time goes in v1:
time: 471 us; the launch traced here: 470 us
  waiting for transfers between devices  194 us (41%)
  blocking collectives  176 us (37%)
  starting transfers between devices  46.2 us (10%)
  matrix products  14.6 us (3%)
  between operations  14.3 us (3%)
  local copies, waits for them, and re-layouts  13.3 us (3%)
  other arithmetic  12.5 us (3%)
    psum x1, waiting for transfers between devices, shards(): lax.psum((grad_gate, grad_up, grad_down, grad_left, grad_right, grad_in,...  179 us
    psum x1, blocking collectives, shards(): lax.psum((grad_gate, grad_up, grad_down, grad_left, grad_right, grad_in,...  95 us
    all_gather x1, blocking collectives, shards(): lax.all_gather(down_weight, 'dp', axis=2, tiled=True)  41.4 us
    all_gather x1, blocking collectives, shards(): lax.all_gather(up_weight, 'dp', axis=2, tiled=True)  39.2 us
    all_to_all x1, starting transfers between devices, shards(): lax.all_to_all(dfirst, 'seq', split_axis=0, concat_axis=1, tiled=True)  25 us
    all_to_all x1, starting transfers between devices, shards(): lax.all_to_all(first_mix, 'seq', split_axis=1, concat_axis=0, tiled=True)  14.5 us
  transfers between devices with their start and end apart: 4, of which 3 were waited for; matrix products, arithmetic and copies ran while one was open for 3% of the time, Pallas kernels for 0%

profile of v1, /device:TPU:17, one launch (start us, length us, event | category | flops | bytes accessed | tf_op | source)
XLA Modules:
  0.0 470.4 jit_solution(11790846292883125581)
XLA Ops:
  7.2 0.9 copy-done
  8.1 1.2 fusion.8
  9.3 0.5 copy.61
  9.8 0.5 broadcast.187
  10.3 1.8 reduce.5
  12.1 0.8 reshape.336
  12.9 14.5 %all-to-all-start = ((bf16[64,2,768]{2,1,0:T(2,128)(2,1)}), bf16[64,2,768]{2,1,0:T(2,128)(2,1)S(1)}, u32[]{:S(2)}, u32[]{:S(2)}) async-start(bf16[64,2,768]{2,1,0:T(2,128)(2,1)} %reshape.336), calls=%async_computation | async-start | bytes 393216 | tf_op jit(solution)/shard_map/all_to_all | solution.py:48
  27.5 0.9 copy.63
  28.4 0.8 convert_element_type.81
  29.3 41.4 %all_gather.7 = bf16[4,96,384]{1,2,0:T(8,128)(2,1)S(1)} all-gather(bf16[4,96,48]{1,2,0:T(8,128)(2,1)S(1)} %copy-done.8), channel_id=1, replica_groups=mesh['dp'=8,'seq'=64] {'dp'}, dimensions={2}, use_global_device_ids=true | all-gather | bytes 331776 | tf_op jit(solution)/shard_map/all_gather | solution.py:37
  70.9 0.3 convolution_bitcast_fusion
  71.4 1.6 copy.74
  73.0 39.2 %all_gather.6 = bf16[4,96,384]{1,2,0:T(8,128)(2,1)S(1)} all-gather(bf16[4,96,48]{1,2,0:T(8,128)(2,1)S(1)} %copy-done.9), channel_id=1, replica_groups=mesh['dp'=8,'seq'=64] {'dp'}, dimensions={2}, use_global_device_ids=true | all-gather | bytes 331776 | tf_op jit(solution)/shard_map/all_gather | solution.py:36
  112.2 0.8 stack.2
  113.0 6.6 %all-to-all-start.1 = ((bf16[8,4,96,48]{2,3,1,0:T(8,128)(2,1)}), bf16[8,4,96,48]{2,3,1,0:T(8,128)(2,1)S(1)}, u32[]{:S(2)}, u32[]{:S(2)}) async-start(bf16[8,4,96,48]{2,3,1,0:T(8,128)(2,1)} %stack.2), calls=%async_computation.1 | async-start | bytes 786432 | tf_op jit(solution)/shard_map/all_to_all | solution.py:10
  119.8 1.1 bitcast_reduce_fusion
  121.3 0.3 reshape.313
  121.6 0.2 copy.64
  121.9 1.9 multiply_convert_fusion.2
  123.8 1.6 fusion.30
  125.4 5.9 %all-to-all-done.1 = bf16[8,4,96,48]{2,3,1,0:T(8,128)(2,1)S(1)} async-done(((bf16[8,4,96,48]{2,3,1,0:T(8,128)(2,1)}), bf16[8,4,96,48]{2,3,1,0:T(8,128)(2,1)S(1)}, u32[]{:S(2)}, u32[]{:S(2)}) %all-to-all-start.1) | async-done | bytes 294944 | tf_op jit(solution)/shard_map/all_to_all | solution.py:10
  131.3 3.8 multiply_convert_fusion
  135.1 0.4 fusion.31
  135.5 1.3 fusion.32
  136.8 1.3 fusion.33
  138.2 0.5 multiply_reduce_fusion
  138.7 0.9 copy.77
  139.6 1.4 copy.67
  141.0 0.3 fusion.19
  141.3 0.9 copy.70
  142.3 0.2 copy.78
  142.6 0.3 reshape.322
  142.8 1.2 multiply_reduce_fusion.1
  144.0 0.2 fusion.9
  144.3 0.8 copy.80
  145.1 25.0 %all-to-all-start.2 = ((bf16[64,4,384]{2,1,0:T(4,128)(2,1)}), bf16[64,4,384]{2,1,0:T(4,128)(2,1)S(1)}, u32[]{:S(2)}, u32[]{:S(2)}) async-start(bf16[64,4,384]{2,1,0:T(4,128)(2,1)} %copy.80), calls=%async_computation.2 | async-start | bytes 393216 | tf_op jit(solution)/shard_map/all_to_all | solution.py:97
  170.4 1.3 fusion.10
  171.7 8.6 %all-to-all-done.2 = bf16[64,4,384]{2,1,0:T(4,128)(2,1)S(1)} async-done(((bf16[64,4,384]{2,1,0:T(4,128)(2,1)}), bf16[64,4,384]{2,1,0:T(4,128)(2,1)S(1)}, u32[]{:S(2)}, u32[]{:S(2)}) %all-to-all-start.2) | async-done | bytes 196640 | tf_op jit(solution)/shard_map/all_to_all | solution.py:97
  180.3 1.0 fusion.25
  181.4 1.0 fusion.18
  182.5 95.0 %all-reduce = (f32[64,64]{1,0:T(8,128)S(1)}, f32[384]{0:T(512)S(1)}, f32[384]{0:T(512)S(1)}, f32[384]{0:T(512)S(1)}) all-reduce(f32[64,64]{1,0:T(8,128)S(1)} %convolution_bitcast_fusion.1, f32[384]{0:T(512)S(1)} %fusion.12, f32[384]{0:T(512)S(1)} %get-tuple-element.20, ...), channel_id=1, replica_groups=mesh['dp'=8,'seq'=64] {'dp','seq'}, use_global_device_ids=true, to_apply=%region_3.0 | all-reduce | flops 5248 | bytes 41984 | tf_op jit(solution)/shard_map/psum | solution.py:104
  277.5 0.6 broadcast_multiply_fusion.4
  278.1 0.6 broadcast_multiply_fusion.2
  278.7 0.6 broadcast_multiply_fusion.1
  279.3 179.4 %all-reduce.4.cloned.1.call-done = (f32[256,256]{1,0:T(8,128)}, f32[4,96,384]{1,2,0:T(8,128)}, f32[4,96,384]{1,2,0:T(8,128)}, f32[4,96,384]{1,2,0:T(8,128)}) async-done(((f32[256,256]{1,0:T(8,128)}, f32[4,96,384]{1,2,0:T(8,128)}, f32[4,96,384]{1,2,0:T(8,128)}, f32[4,96,384]{1,2,0:T(8,128)}), (f32[256,256]{1,0:T(8,128)}, f32[4,96,384]{1,2,0:T(8,128)}, f32[4,96,384]{1,2,0:T(8,128)}, ...) | async-done | bytes 2031632 | tf_op jit(solution)/shard_map/psum | solution.py:104
  458.7 1.7 broadcast_multiply_fusion
  460.4 1.5 dynamic-slice_multiply_fusion.2
  461.9 1.6 dynamic-slice_multiply_fusion
  (45 shorter events, 1.8 us)
Async XLA Ops:
  7.2 0.9 copy-start
  7.2 20.3 %copy-start.1 = (bf16[1,256,384]{2,1,0:T(8,128)(2,1)S(1)}, bf16[1,256,384]{2,1,0:T(8,128)(2,1)}, u32[]{:S(2)}) copy-start(bf16[1,256,384]{2,1,0:T(8,128)(2,1)} %param.10) | copy-start | bytes 589828
  9.3 19.9 %copy-start.12 = (f32[384]{0:T(512)S(1)}, f32[384]{0:T(512)}, u32[]{:S(2)}) copy-start(f32[384]{0:T(512)} %param.16) | copy-start | bytes 4612
  9.3 19.9 %copy-start.6 = (f32[384]{0:T(512)S(1)}, f32[384]{0:T(512)}, u32[]{:S(2)}) copy-start(f32[384]{0:T(512)} %param.13) | copy-start | bytes 4612
  9.3 20.0 %copy-start.8 = (bf16[4,96,48]{1,2,0:T(8,128)(2,1)S(1)}, bf16[4,96,48]{1,2,0:T(8,128)(2,1)}, u32[]{:S(2)}) copy-start(bf16[4,96,48]{1,2,0:T(8,128)(2,1)} %param.19) | copy-start | bytes 110596
  9.8 61.0 %copy-start.2 = (bf16[1,256,384]{2,1,0:T(8,128)(2,1)S(1)}, bf16[1,256,384]{2,1,0:T(8,128)(2,1)}, u32[]{:S(2)}) copy-start(bf16[1,256,384]{2,1,0:T(8,128)(2,1)} %param.11) | copy-start | bytes 589828
  12.9 99.3 %all-to-all-start = ((bf16[64,2,768]{2,1,0:T(2,128)(2,1)}), bf16[64,2,768]{2,1,0:T(2,128)(2,1)S(1)}, u32[]{:S(2)}, u32[]{:S(2)}) async-start(bf16[64,2,768]{2,1,0:T(2,128)(2,1)} %reshape.336), calls=%async_computation | async-start | bytes 393216 | tf_op jit(solution)/shard_map/all_to_all | solution.py:48
  71.4 1.7 copy-start.9
  71.4 40.8 %copy-start.10 = (bf16[4,96,48]{1,2,0:T(8,128)(2,1)S(1)}, bf16[4,96,48]{1,2,0:T(8,128)(2,1)}, u32[]{:S(2)}) copy-start(bf16[4,96,48]{1,2,0:T(8,128)(2,1)} %param.17) | copy-start | bytes 110596
  73.0 47.9 %copy-start.7 = (bf16[64,64]{1,0:T(8,128)(2,1)S(1)}, bf16[64,64]{1,0:T(8,128)(2,1)}, u32[]{:S(2)}) copy-start(bf16[64,64]{1,0:T(8,128)(2,1)} %param.15) | copy-start | bytes 24580
  113.0 18.3 %all-to-all-start.1 = ((bf16[8,4,96,48]{2,3,1,0:T(8,128)(2,1)}), bf16[8,4,96,48]{2,3,1,0:T(8,128)(2,1)S(1)}, u32[]{:S(2)}, u32[]{:S(2)}) async-start(bf16[8,4,96,48]{2,3,1,0:T(8,128)(2,1)} %stack.2), calls=%async_computation.1 | async-start | bytes 786432 | tf_op jit(solution)/shard_map/all_to_all | solution.py:10
  135.5 2.7 copy-start.5
  145.1 35.2 %copy-start.11 = (f32[384]{0:T(512)S(1)}, f32[384]{0:T(512)}, u32[]{:S(2)}) copy-start(f32[384]{0:T(512)} %param.12) | copy-start | bytes 4612
  145.1 35.1 %all-to-all-start.2 = ((bf16[64,4,384]{2,1,0:T(4,128)(2,1)}), bf16[64,4,384]{2,1,0:T(4,128)(2,1)S(1)}, u32[]{:S(2)}, u32[]{:S(2)}) async-start(bf16[64,4,384]{2,1,0:T(4,128)(2,1)} %copy.80), calls=%async_computation.2 | async-start | bytes 393216 | tf_op jit(solution)/shard_map/all_to_all | solution.py:97
  170.1 288.6 %all-reduce.4.cloned.1.call-start = ((), (), s32[]{:S(2)}) async-start(), calls=%async_computation.3 | async-start | bytes 5242880 | tf_op jit(solution)/shard_map/psum | solution.py:104
  180.3 1.0 copy-start.3
  180.3 1.1 copy-start.4
Sparse Core Ops, SparseCore 0:
  181.4 277.2 all-reduce.3
